TPU v7x, 512 devices: a whole 4x4x16 slice. The times are simulated.
512 devices in a mesh: grid: 128 (over y, z, core), bundle: 4 (over x).
Axes of the slice: x: 4, y: 4, z: 16, core: 2. Of those that a mesh axis runs over, the one named last changes fastest.
Arguments:
- cell_state: float32 [24, 524288], P(None, 'grid'), may hold values from -6 to 6
- pore_volume: float32 [524288], P('grid'), may hold values from 0.5 to 5
- request_cell: int32 [4, 128, 128, 32], P(None, 'grid'), may hold values from 0 to 4095, as said below
- node_slot: int32 [4, 256, 2048], P('bundle', 'grid'), may hold values from 0 to 4095, as said below
- line_length: int32 [4, 256], P('bundle', 'grid'), may hold values from 128 to 2048, as said below
- courant: float32 [4, 256, 2048], P('bundle', 'grid'), may hold values from 0.3 to 3
- flux_weight: float32 [4, 256, 2048], P('bundle', 'grid'), may hold values from 0.3 to 3
- inflow: float32 [4, 24], P('bundle'), may hold values from -4 to 4
- interaction: float32 [24, 24], replicated, may hold values from -0.18 to 0.18
Outputs:
- new_state: float32 [24, 524288], P(None, 'grid')
Inputs may be any that keep to these rules, and one draw needn't show every extreme that they name: `request_cell`: a cell owner's local cell index; one entry is the last cell. `node_slot`: an index into the 4096 slots of the device that holds the streamline, slot o * 32 + c belonging to owner o; the last slot is used. `line_length`: live nodes come first on each streamline; some streamline has 2048 and some has 128.
All inputs are finite; a program needn't handle non-finite values.
Results may differ from a plain program's by a relative error of at most 0.0001.
Values sent between devices are 32-bit elements; how exact they have to be, the bound alone decides.
A program may use at most 64 MiB of HBM per device.

v0:
```python
import jax
import jax.numpy as jnp
from jax import lax
from jax.experimental import pallas as pl
from jax.experimental.pallas import tpu as pltpu
from jax.sharding import PartitionSpec as P

SUB = 2
NEWTON = 3
SPECIES = 24
CELLS = 4096
SLOTS = 4096
NODES = 2048
LINES = 2
GRID = 128
BUNDLES = 4
CAP = 32
CHUNKS = 64
STEPS = NODES // CHUNKS
TILES = 32
LANES = 128
LOW = 256
HIGH = 16
QUARTER = CELLS // BUNDLES
MESH = pl.DeviceIdType.MESH


def lane_ids(rows):
    return lax.broadcasted_iota(jnp.int32, (rows, LANES), 1)


def row_ids(rows=8):
    return lax.broadcasted_iota(jnp.int32, (rows, LANES), 0)


def swap_blocks(parts):
    lane = lane_ids(parts[0].shape[0])
    far = lane < 64
    near = (lane & 32) == 0
    a, b, c, d = parts
    a, c = jnp.where(far, a, pltpu.roll(c, 64, 1)), jnp.where(far, pltpu.roll(a, 64, 1), c)
    b, d = jnp.where(far, b, pltpu.roll(d, 64, 1)), jnp.where(far, pltpu.roll(b, 64, 1), d)
    a, b = jnp.where(near, a, pltpu.roll(b, 32, 1)), jnp.where(near, pltpu.roll(a, 96, 1), b)
    c, d = jnp.where(near, c, pltpu.roll(d, 32, 1)), jnp.where(near, pltpu.roll(c, 96, 1), d)
    return a, b, c, d


def to_groups(v0, v1, v2):
    row = row_ids()
    last = jnp.where(
        row < 2,
        pltpu.roll(v0, 2, 0),
        jnp.where(row < 4, pltpu.roll(v1, 4, 0), pltpu.roll(v2, 6, 0)),
    )
    return v0, v1, v2, last


def from_groups(g0, g1, g2, g3):
    row = row_ids()
    low = row < 6
    return (
        jnp.where(low, g0, pltpu.roll(g3, 6, 0)),
        jnp.where(low, g1, pltpu.roll(g3, 4, 0)),
        jnp.where(low, g2, pltpu.roll(g3, 2, 0)),
    )


def gather_tile(load, index):
    lane = jnp.broadcast_to(index & 127, (8, LANES))
    tile = jnp.broadcast_to(index >> 7, (8, LANES))
    found = [jnp.zeros((8, LANES), jnp.float32)] * 3
    for k in range(TILES):
        here = tile == k
        for g in range(3):
            found[g] = jnp.where(here, jnp.take_along_axis(load(k, g), lane, axis=1), found[g])
    return found


def scatter_sums(rows_ref, index_ref, acc_ref):
    width = 512
    acc_ref[...] = jnp.zeros_like(acc_ref)

    def step(j, _):
        off = pl.multiple_of(j * width, width)
        index = index_ref[:, pl.ds(off, width)]
        rows = rows_ref[:, pl.ds(off, width)]
        top = rows.astype(jnp.bfloat16).astype(jnp.float32)
        rest = rows - top
        high = index >> 8
        tops = []
        rests = []
        for k in range(HIGH):
            here = jnp.broadcast_to(high == k, (32, width))
            tops.append(jnp.where(here, top, 0.0).astype(jnp.bfloat16))
            rests.append(jnp.where(here, rest, 0.0).astype(jnp.bfloat16))
        left = jnp.concatenate([jnp.concatenate(tops, 0), jnp.concatenate(rests, 0)], 1)
        low = jnp.broadcast_to(index & (LOW - 1), (LOW, width))
        hot = lax.broadcasted_iota(jnp.int32, (LOW, width), 0) == low
        hot = hot.astype(jnp.float32).astype(jnp.bfloat16)
        right = jnp.concatenate([hot, hot], 1)
        acc_ref[...] += lax.dot_general(
            left, right, (((1,), (1,)), ((), ())), preferred_element_type=jnp.float32
        )
        return 0

    lax.fori_loop(0, rows_ref.shape[1] // width, step, 0)


def kernel(
    cell_ref,
    pore_ref,
    request_ref,
    slot_ref,
    courant_ref,
    weight_ref,
    inflow_ref,
    inter_ref,
    out_ref,
    send1,
    recv1,
    send2,
    recv2,
    table,
    state,
    rows,
    acc,
    part,
    part_flux,
    got,
    got_flux,
    own_sem,
    send1_sem,
    recv1_sem,
    send2_sem,
    recv2_sem,
    send3_sem,
    recv3_sem,
    send4_sem,
    recv4_sem,
    send5_sem,
    recv5_sem,
):
    me = lax.axis_index("grid")
    mine = lax.axis_index("bundle")

    barrier = pltpu.get_barrier_semaphore()

    def greet(k, _):
        pl.semaphore_signal(
            barrier, inc=1, device_id=(lax.rem(me + k, GRID), mine), device_id_type=MESH
        )
        return 0

    lax.fori_loop(1, GRID, greet, 0)
    for k in range(1, BUNDLES):
        pl.semaphore_signal(
            barrier, inc=1, device_id=(me, lax.rem(mine + k, BUNDLES)), device_id_type=MESH
        )

    def pick(t, _):
        index = request_ref[:, pl.ds(pl.multiple_of(t * LANES, LANES), LANES)]
        found = gather_tile(
            lambda k, g: cell_ref[8 * g : 8 * g + 8, k * LANES : (k + 1) * LANES], index
        )
        blocks = swap_blocks(to_groups(*found))
        for d in range(4):
            send1[t * 4 + d] = blocks[d][:6]
        return 0

    lax.fori_loop(0, TILES, pick, 0)
    pl.semaphore_wait(barrier, GRID - 1 + BUNDLES - 1)

    def exchange(source, target, send_sem, recv_sem):
        def post(k, _):
            peer = lax.rem(me + k, GRID)
            pltpu.make_async_remote_copy(
                src_ref=source.at[peer],
                dst_ref=target.at[me],
                send_sem=send_sem,
                recv_sem=recv_sem,
                device_id=(peer, mine),
                device_id_type=MESH,
            ).start()
            return 0

        lax.fori_loop(1, GRID, post, 0)
        own = pltpu.make_async_copy(source.at[me], target.at[me], own_sem)
        own.start()
        own.wait()

    def settle(source, target, send_sem, recv_sem):
        rest = pl.ds(0, GRID - 1)
        pltpu.make_async_copy(target.at[rest], target.at[rest], recv_sem).wait()
        pltpu.make_async_copy(source.at[rest], source.at[rest], send_sem).wait()

    exchange(send1, recv1, send1_sem, recv1_sem)
    settle(send1, recv1, send1_sem, recv1_sem)

    def unpack(t, _):
        pad = jnp.zeros((2, LANES), jnp.float32)
        parts = swap_blocks([jnp.concatenate([recv1[t * 4 + d], pad], 0) for d in range(4)])
        for g, value in enumerate(from_groups(*parts)):
            table[t, 8 * g : 8 * g + 8, :] = value
        return 0

    lax.fori_loop(0, TILES, unpack, 0)

    def fetch(t, _):
        index = slot_ref[:, pl.ds(pl.multiple_of(t * LANES, LANES), LANES)]
        found = gather_tile(lambda k, g: table[k, 8 * g : 8 * g + 8, :], index)
        for g in range(3):
            state[t, 8 * g : 8 * g + 8, :] = found[g]
        return 0

    lax.fori_loop(0, TILES, fetch, 0)

    chunk = lane_ids(SPECIES) & (CHUNKS - 1)
    entry = inflow_ref[...]

    def rate(i):
        return courant_ref[:, i * LANES : (i + 1) * LANES]

    scales = []
    decays = []
    spans = []
    for i in range(STEPS):
        scale = 1.0 / (1.0 + rate(i))
        decay = rate(i) * scale
        scales.append(jnp.broadcast_to(scale, (8, LANES)))
        decays.append(jnp.broadcast_to(decay, (8, LANES)))
        spans.append(decays[0] if i == 0 else spans[-1] * decays[i])
    wide = [[jnp.concatenate([x] * 3, 0) for x in xs] for xs in (scales, decays, spans)]
    scales, decays, spans = wide
    levels = []
    level = spans[-1]
    for bit in range(6):
        levels.append(level)
        behind = pltpu.roll(level, 1 << bit, 1)
        level = jnp.where(chunk >= (1 << bit), level * behind, level)
    for substep in range(SUB):
        value = jnp.zeros((SPECIES, LANES), jnp.float32)
        for i in range(STEPS):
            value = decays[i] * value + scales[i] * state[i]
            state[i] = value
        ends = jnp.where(chunk == 0, value + spans[-1] * entry, value)
        for bit in range(6):
            behind = pltpu.roll(ends, 1 << bit, 1)
            ends = jnp.where(chunk >= (1 << bit), ends + levels[bit] * behind, ends)
        before = jnp.where(chunk == 0, entry, pltpu.roll(ends, 1, 1))
        for i in range(STEPS):
            state[i] = state[i] + spans[i] * before

    inter = inter_ref[...]

    def react(j, _):
        base = jnp.concatenate([state[j * 4 + q] for q in range(4)], 1)
        iterate = base
        for _step in range(NEWTON):
            iterate = base - jnp.dot(
                inter,
                jnp.tanh(iterate),
                precision=lax.Precision.HIGHEST,
                preferred_element_type=jnp.float32,
            )
        for q in range(4):
            off = pl.multiple_of((j * 4 + q) * LANES, LANES)
            weight = jnp.broadcast_to(weight_ref[:, pl.ds(off, LANES)], (8, LANES))
            result = iterate[:, q * LANES : (q + 1) * LANES]
            groups = to_groups(*[result[8 * g : 8 * g + 8] * weight for g in range(3)])
            groups = (jnp.where(row_ids() == 6, weight, groups[0]),) + groups[1:]
            for g in range(4):
                rows[8 * g : 8 * g + 8, pl.ds(off, LANES)] = groups[g]
        return 0

    lax.fori_loop(0, TILES // 4, react, 0)
    scatter_sums(rows, slot_ref, acc)

    def pack(h, _):
        for half in range(2):
            parts = [
                acc[pl.ds(pl.multiple_of(h * 32 + 8 * g, 8), 8), half * LANES : (half + 1) * LANES]
                for g in range(4)
            ]
            blocks = swap_blocks(parts)
            for d in range(4):
                send2[h * 8 + half * 4 + d] = blocks[d][:7]
        return 0

    lax.fori_loop(0, HIGH, pack, 0)
    exchange(send2, recv2, send2_sem, recv2_sem)
    settle(send2, recv2, send2_sem, recv2_sem)

    def unpack_back(t, _):
        off = pl.multiple_of(t * LANES, LANES)
        pad = jnp.zeros((1, LANES), jnp.float32)
        parts = swap_blocks([jnp.concatenate([recv2[t * 4 + d], pad], 0) for d in range(4)])
        for g in range(4):
            rows[8 * g : 8 * g + 8, pl.ds(off, LANES)] = parts[g]
        return 0

    lax.fori_loop(0, TILES, unpack_back, 0)
    scatter_sums(rows, request_ref, acc)

    for h in range(HIGH):
        for half in range(2):
            lanes = slice(half * LANES, (half + 1) * LANES)
            groups = [acc[h * 32 + 8 * g : h * 32 + 8 * g + 8, lanes] for g in range(4)]
            cells = slice((h * 2 + half) * LANES, (h * 2 + half + 1) * LANES)
            for g, value in enumerate(from_groups(*groups)):
                part[8 * g : 8 * g + 8, cells] = value
            part_flux[:, cells] = groups[0][6:7]

    posts = []
    for k in range(1, BUNDLES):
        peer = lax.rem(mine + k, BUNDLES)
        cells = pl.ds(pl.multiple_of(peer * QUARTER, QUARTER), QUARTER)
        for source, target, sends, recvs in (
            (part, got, send3_sem, recv3_sem),
            (part_flux, got_flux, send4_sem, recv4_sem),
        ):
            copy = pltpu.make_async_remote_copy(
                src_ref=source.at[:, cells],
                dst_ref=target.at[k - 1],
                send_sem=sends.at[k - 1],
                recv_sem=recvs.at[k - 1],
                device_id=(me, peer),
                device_id_type=MESH,
            )
            copy.start()
            posts.append(copy)
    for copy in posts:
        copy.wait()
    ours = pl.ds(pl.multiple_of(mine * QUARTER, QUARTER), QUARTER)
    total = part[:, ours] + got[0] + got[1] + got[2]
    flux = part_flux[:, ours] + got_flux[0] + got_flux[1] + got_flux[2]
    pore = pore_ref[:, ours]
    out_ref[:, ours] = (pore * cell_ref[:, ours] + total) / (pore + flux)
    posts = []
    for k in range(1, BUNDLES):
        copy = pltpu.make_async_remote_copy(
            src_ref=out_ref.at[:, ours],
            dst_ref=out_ref.at[:, ours],
            send_sem=send5_sem.at[k - 1],
            recv_sem=recv5_sem.at[k - 1],
            device_id=(me, lax.rem(mine + k, BUNDLES)),
            device_id_type=MESH,
        )
        copy.start()
        posts.append(copy)
    for copy in posts:
        copy.wait()


def by_step(values):
    return values.reshape(LINES, CHUNKS, STEPS).transpose(2, 0, 1).reshape(1, LINES * NODES)


def shards(
    cell_state,
    pore_volume,
    request_cell,
    node_slot,
    line_length,
    courant,
    flux_weight,
    inflow,
    interaction,
):
    request = lax.dynamic_index_in_dim(
        request_cell[:, 0], lax.axis_index("bundle"), 0, keepdims=False
    ).reshape(1, SLOTS)
    positions = lax.broadcasted_iota(jnp.int32, (LINES, NODES), 1)
    weight = jnp.where(positions < line_length[0][:, None], flux_weight[0], 0.0)
    entry = jnp.broadcast_to(inflow[0][:, None], (SPECIES, LANES))
    vmem = pl.BlockSpec(memory_space=pltpu.VMEM)
    f32 = jnp.float32
    dma = pltpu.SemaphoreType.DMA
    return pl.pallas_call(
        kernel,
        out_shape=jax.ShapeDtypeStruct((SPECIES, CELLS), f32),
        in_specs=[vmem] * 8,
        out_specs=vmem,
        scratch_shapes=[
            pltpu.VMEM((GRID, 6, LANES), f32),
            pltpu.VMEM((GRID, 6, LANES), f32),
            pltpu.VMEM((GRID, 7, LANES), f32),
            pltpu.VMEM((GRID, 7, LANES), f32),
            pltpu.VMEM((TILES, SPECIES, LANES), f32),
            pltpu.VMEM((TILES, SPECIES, LANES), f32),
            pltpu.VMEM((32, SLOTS), f32),
            pltpu.VMEM((HIGH * 32, LOW), f32),
            pltpu.VMEM((SPECIES, CELLS), f32),
            pltpu.VMEM((1, CELLS), f32),
            pltpu.VMEM((BUNDLES - 1, SPECIES, QUARTER), f32),
            pltpu.VMEM((BUNDLES - 1, 1, QUARTER), f32),
            dma,
            dma,
            dma,
            dma,
            dma,
            dma((3,)),
            dma((3,)),
            dma((3,)),
            dma((3,)),
            dma((3,)),
            dma((3,)),
        ],
        compiler_params=pltpu.CompilerParams(collective_id=0, has_side_effects=True),
        name="streamlines",
    )(
        cell_state,
        pore_volume.reshape(1, CELLS),
        request,
        by_step(node_slot),
        by_step(courant),
        by_step(weight),
        entry,
        interaction,
    )


def solution(mesh):
    placed = (
        P(None, "grid"),
        P("grid"),
        P(None, "grid", None, None),
        P("bundle", "grid", None),
        P("bundle", "grid"),
        P("bundle", "grid", None),
        P("bundle", "grid", None),
        P("bundle", None),
        P(),
    )
    return jax.shard_map(
        shards, mesh=mesh, in_specs=placed, out_specs=P(None, "grid"), check_vma=False
    )
```

profile of v0, /device:TPU:1, one launch (start us, length us, event | category | flops | bytes accessed | tf_op | source)
XLA Modules:
  0.0 118.2 jit_solution(7648143950482738873)
XLA Ops:
  0.0 0.0 copy-start
  0.0 0.0 copy-start.5
  0.0 0.7 copy-done.5
  0.7 0.7 broadcast_in_dim.13.inflow_ref
  1.4 0.0 copy-done
  1.4 0.1 copy.14
  1.5 0.0 copy-start.1
  1.5 0.7 reshape.43.request_ref
  2.2 0.0 copy-done.1
  2.2 0.1 reshape.44
  2.3 0.1 copy.15
  2.4 0.7 reshape.45.slot_ref
  3.1 0.0 copy-done.2
  3.1 0.1 reshape.46
  3.2 0.1 copy.16
  3.3 0.7 reshape.47.courant_ref
  4.0 0.0 copy-done.3
  4.0 0.1 squeeze.6
  4.1 0.6 copy-done.4
  4.7 0.1 select_bitcast_fusion
  4.7 0.1 copy.17
  4.8 0.7 reshape.48.weight_ref
  5.5 110.9 %streamlines.1 = f32[24,4096]{1,0:T(8,128)} custom-call(f32[24,4096]{1,0:T(8,128)} %cell_ref.1, f32[1,4096]{1,0:T(1,128)} %bitcast.11, s32[1,4096]{1,0:T(1,128)} %reshape.43.request_ref, s32[1,4096]{1,0:T(1,128)} %reshape.45.slot_ref, f32[1,4096]{1,0:T(1,128)} %reshape.47.courant_ref, f32[1,4096]{1,0:T(1,128)} %reshape.48.weight_ref, ...), custom_call_target="tpu_custom_call" | custom-call | tf_op jit(solution)/shard_map/streamlines/pallas_call | solution.py:378
  116.5 1.8 %copy.19 = f32[24,4096]{1,0:T(8,128)} copy(f32[24,4096]{1,0:T(8,128)} %streamlines.1) | data formatting | bytes 786432
  (5 shorter events, 0.0 us)
Async XLA Ops:
  0.0 1.4 %copy-start = (s32[4,1,128,32]{2,3,1,0:T(8,128)S(1)}, s32[4,1,128,32]{2,3,1,0:T(8,128)}, u32[]{:S(2)}) copy-start(s32[4,1,128,32]{2,3,1,0:T(8,128)} %param.11) | copy-start | bytes 196612
  0.0 0.7 copy-start.5
  1.5 0.7 copy-start.1
  2.4 0.7 copy-start.2
  3.3 0.7 copy-start.3
  4.0 0.7 copy-start.4
where the time goes:
time: 119 us; the launch traced here: 118 us
  Pallas kernels  111 us (93%)
  local copies, waits for them, and re-layouts  7.14 us (6%)
    pallas_call x1, Pallas kernels, shards(): pl.pallas_call(kernel, out_shape=jax.ShapeDtypeStruct((SPECIES, CELLS), f...  111 us
    unnamed x13, local copies, waits for them, and re-layouts  3.07 us

commit v1 on v0

v1 whole, which is shorter than its diff:
```python
import jax
import jax.numpy as jnp
from jax import lax
from jax.experimental import pallas as pl
from jax.experimental.pallas import tpu as pltpu
from jax.sharding import PartitionSpec as P

SUB = 2
NEWTON = 3
SPECIES = 24
CELLS = 4096
SLOTS = 4096
NODES = 2048
LINES = 2
GRID = 128
BUNDLES = 4
CAP = 32
CHUNKS = 64
STEPS = NODES // CHUNKS
TILES = 32
LANES = 128
LOW = 256
HIGH = 16
QUARTER = CELLS // BUNDLES
MESH = pl.DeviceIdType.MESH


def lane_ids(rows):
    return lax.broadcasted_iota(jnp.int32, (rows, LANES), 1)


def row_ids(rows=8):
    return lax.broadcasted_iota(jnp.int32, (rows, LANES), 0)


def swap_blocks(parts):
    lane = lane_ids(parts[0].shape[0])
    far = lane < 64
    near = (lane & 32) == 0
    a, b, c, d = parts
    a, c = jnp.where(far, a, pltpu.roll(c, 64, 1)), jnp.where(far, pltpu.roll(a, 64, 1), c)
    b, d = jnp.where(far, b, pltpu.roll(d, 64, 1)), jnp.where(far, pltpu.roll(b, 64, 1), d)
    a, b = jnp.where(near, a, pltpu.roll(b, 32, 1)), jnp.where(near, pltpu.roll(a, 96, 1), b)
    c, d = jnp.where(near, c, pltpu.roll(d, 32, 1)), jnp.where(near, pltpu.roll(c, 96, 1), d)
    return a, b, c, d


def to_groups(v0, v1, v2):
    row = row_ids()
    last = jnp.where(
        row < 2,
        pltpu.roll(v0, 2, 0),
        jnp.where(row < 4, pltpu.roll(v1, 4, 0), pltpu.roll(v2, 6, 0)),
    )
    return v0, v1, v2, last


def from_groups(g0, g1, g2, g3):
    row = row_ids()
    low = row < 6
    return (
        jnp.where(low, g0, pltpu.roll(g3, 6, 0)),
        jnp.where(low, g1, pltpu.roll(g3, 4, 0)),
        jnp.where(low, g2, pltpu.roll(g3, 2, 0)),
    )


def gather_tile(load, index, count, found):
    lane = jnp.broadcast_to(index & 127, (8, LANES))
    tile = jnp.broadcast_to(index >> 7, (8, LANES))
    for k in range(count):
        here = tile == k
        for g in range(3):
            found[g] = jnp.where(here, jnp.take_along_axis(load(k, g), lane, axis=1), found[g])
    return found


def expand(tiles, indices, highs):
    tops = []
    rests = []
    for tile, index in zip(tiles, indices):
        top = tile.astype(jnp.bfloat16).astype(jnp.float32)
        rest = tile - top
        high = jnp.broadcast_to(index >> 8, (32, LANES))
        column = [[], []]
        for k in highs:
            here = high == k
            column[0].append(jnp.where(here, top, 0.0).astype(jnp.bfloat16))
            column[1].append(jnp.where(here, rest, 0.0).astype(jnp.bfloat16))
        tops.append(jnp.concatenate(column[0], 0))
        rests.append(jnp.concatenate(column[1], 0))
    return jnp.concatenate(tops + rests, 1)


def hot_tile(index):
    low = jnp.broadcast_to(index & (LOW - 1), (LOW, LANES))
    hot = lax.broadcasted_iota(jnp.int32, (LOW, LANES), 0) == low
    return hot.astype(jnp.float32).astype(jnp.bfloat16)


def contract(left, hots):
    right = jnp.concatenate(hots + hots, 1)
    return lax.dot_general(
        left, right, (((1,), (1,)), ((), ())), preferred_element_type=jnp.float32
    )


def side_by_side(blocks):
    lane = lane_ids(32)
    out = blocks[0]
    for j in range(1, 4):
        out = jnp.where(lane >= 32 * j, pltpu.roll(blocks[j], 32 * j, 1), out)
    return out


def by_step(source_ref, lines_ref, square_ref):
    for m in range(16):
        lines_ref[2 * m : 2 * m + 2, :] = source_ref[:, m * LANES : (m + 1) * LANES]
    square_ref[:, 0:32] = jnp.transpose(lines_ref[...], (1, 0))
    mixed = side_by_side([square_ref[32 * q : 32 * q + 32, :] for q in range(4)])
    lane = lane_ids(8)
    take = (lane & 3) * 32 + ((lane >> 2) & 15) * 2 + (lane >> 6)
    return jnp.concatenate(
        [jnp.take_along_axis(mixed[8 * j : 8 * j + 8], take, axis=1) for j in range(4)], 0
    )


ORDER = (2, 1, 3, 0)


def kernel(
    cell_hbm,
    pore_hbm,
    request_hbm,
    slot_hbm,
    length_hbm,
    courant_hbm,
    weight_hbm,
    inflow_hbm,
    inter_hbm,
    out_ref,
    cell_ref,
    pore_ref,
    request_in,
    slot_in,
    length_in,
    courant_in,
    weight_in,
    inflow_in,
    inter_in,
    square_i,
    square_f,
    lines_i,
    lines_f,
    request_ref,
    slot_ref,
    weight_ref,
    scale_ref,
    decay_ref,
    span_ref,
    hot_slot,
    hot_request,
    send1,
    recv1,
    send2,
    recv2,
    table,
    state,
    rows,
    acc,
    part,
    part_flux,
    got,
    got_flux,
    in_sem,
    own_sem,
    send1_sem,
    recv1_sem,
    send2_sem,
    recv2_sem,
    send3_sem,
    recv3_sem,
    send4_sem,
    recv4_sem,
    send5_sem,
    recv5_sem,
):
    me = lax.axis_index("grid")
    mine = lax.axis_index("bundle")
    my_y = lax.div(me, 32)
    my_z = lax.rem(lax.div(me, 2), 16)
    my_core = lax.rem(me, 2)

    loads = [
        pltpu.make_async_copy(source, target, in_sem.at[j])
        for j, (source, target) in enumerate(
            (
                (request_hbm.at[mine], request_in),
                (cell_hbm, cell_ref),
                (slot_hbm, slot_in),
                (courant_hbm, courant_in),
                (weight_hbm, weight_in),
                (length_hbm, length_in),
                (inflow_hbm, inflow_in),
                (inter_hbm, inter_in),
                (pore_hbm, pore_ref),
            )
        )
    ]
    for load in loads:
        load.start()

    barrier = pltpu.get_barrier_semaphore()

    def greet(k, _):
        pl.semaphore_signal(
            barrier, inc=1, device_id=(lax.rem(me + k, GRID), mine), device_id_type=MESH
        )
        return 0

    lax.fori_loop(1, GRID, greet, 0)
    for k in range(1, BUNDLES):
        pl.semaphore_signal(
            barrier, inc=1, device_id=(me, lax.rem(mine + k, BUNDLES)), device_id_type=MESH
        )

    loads[0].wait()
    square_i[:, 0:32] = jnp.transpose(request_in[...], (1, 0))
    request_ref[...] = side_by_side([square_i[pl.ds(d, 32, stride=4), :] for d in range(4)])
    loads[1].wait()

    def pick(t, _):
        found = gather_tile(
            lambda k, g: cell_ref[8 * g : 8 * g + 8, k * LANES : (k + 1) * LANES],
            request_ref[pl.ds(t, 1), :],
            TILES,
            [jnp.zeros((8, LANES), jnp.float32)] * 3,
        )
        blocks = swap_blocks(to_groups(*found))
        for d in range(4):
            send1[t * 4 + d] = blocks[d][:6]
        return 0

    lax.fori_loop(0, TILES, pick, 0, unroll=2)
    pl.semaphore_wait(barrier, GRID - 1 + BUNDLES - 1)

    def post_one(source, target, send_sem, recv_sem, peer):
        pltpu.make_async_remote_copy(
            src_ref=source.at[peer],
            dst_ref=target.at[me],
            send_sem=send_sem,
            recv_sem=recv_sem,
            device_id=(peer, mine),
            device_id_type=MESH,
        ).start()

    def post(source, target, send_sem, recv_sems, r):
        first = lax.rem(my_y + r, 4) * 32

        def ring(j, _):
            hop = 8 + lax.div(j + 1, 2) * (1 - 2 * lax.rem(j, 2))
            spot = first + lax.rem(my_z + hop, 16) * 2
            for core in range(2):
                post_one(source, target, send_sem, recv_sems.at[r], spot + core)
            return 0

        lax.fori_loop(0, 16 if r else 15, ring, 0)
        if r == 0:
            post_one(
                source, target, send_sem, recv_sems.at[0], first + my_z * 2 + 1 - my_core
            )
            own = pltpu.make_async_copy(source.at[me], target.at[me], own_sem)
            own.start()
            own.wait()

    def arrived(target, recv_sems, r):
        blocks = pl.ds(0, 32 if r else 31)
        pltpu.make_async_copy(target.at[blocks], target.at[blocks], recv_sems.at[r]).wait()
        return lax.rem(my_y + 4 - r, 4)

    def sent(source, send_sem):
        blocks = pl.ds(0, GRID - 1)
        pltpu.make_async_copy(source.at[blocks], source.at[blocks], send_sem).wait()

    for r in ORDER:
        post(send1, recv1, send1_sem, recv1_sem, r)

    for load in loads[2:]:
        load.wait()
    slot_ref[...] = by_step(slot_in, lines_i, square_i)
    courant = by_step(courant_in, lines_f, square_f)
    scale = 1.0 / (1.0 + courant)
    scale_ref[...] = scale
    decay_ref[...] = courant * scale
    span_ref[0:1, :] = decay_ref[0:1, :]
    for i in range(1, STEPS):
        span_ref[i : i + 1, :] = span_ref[i - 1 : i, :] * decay_ref[i : i + 1, :]
    flux = by_step(weight_in, lines_f, square_f)
    lane = lane_ids(32)
    node = (lane & (CHUNKS - 1)) * STEPS + row_ids(32)
    first_line = jnp.broadcast_to(length_in[:, 0:1], (32, LANES))
    second_line = jnp.broadcast_to(length_in[:, 1:2], (32, LANES))
    weight_ref[...] = jnp.where(node < jnp.where(lane < CHUNKS, first_line, second_line), flux, 0.0)

    def heat(t, _):
        hot_slot[t] = hot_tile(slot_ref[pl.ds(t, 1), :])
        hot_request[t] = hot_tile(request_ref[pl.ds(t, 1), :])
        return 0

    lax.fori_loop(0, TILES, heat, 0)
    square = lax.broadcasted_iota(jnp.int32, (SPECIES, SPECIES), 0) == lax.broadcasted_iota(
        jnp.int32, (SPECIES, SPECIES), 1
    )
    entry = jnp.sum(
        jnp.where(square, jnp.broadcast_to(inflow_in[...], (SPECIES, SPECIES)), 0.0),
        axis=1,
        keepdims=True,
    )
    entry = jnp.broadcast_to(entry, (SPECIES, LANES))
    square_f[0:SPECIES, :] = jnp.zeros((SPECIES, LANES), jnp.float32)
    square_f[0:SPECIES, 0:SPECIES] = inter_in[...]
    inter = square_f[0:SPECIES, :]
    inter_top = inter.astype(jnp.bfloat16).astype(jnp.float32)
    inter_rest = inter - inter_top
    inter = inter_top + pltpu.roll(inter_top, 32, 1) + pltpu.roll(inter_rest, 64, 1)
    inter = inter.astype(jnp.bfloat16)
    chunk = lane_ids(SPECIES) & (CHUNKS - 1)
    levels = []
    level = jnp.broadcast_to(span_ref[STEPS - 1 : STEPS, :], (SPECIES, LANES))
    span_all = level
    for bit in range(6):
        levels.append(level)
        behind = pltpu.roll(level, 1 << bit, 1)
        level = jnp.where(chunk >= (1 << bit), level * behind, level)

    for step, r in enumerate(ORDER):
        base = arrived(recv1, recv1_sem, r) * 8
        pad = jnp.zeros((2, LANES), jnp.float32)
        for u in range(8):
            parts = [
                jnp.concatenate([recv1[base * 4 + u * 4 + d], pad], 0) for d in range(4)
            ]
            for g, value in enumerate(from_groups(*swap_blocks(parts))):
                table[u, 8 * g : 8 * g + 8, :] = value

        def fetch(t, _, base=base, step=step):
            if step == 0:
                found = [jnp.zeros((8, LANES), jnp.float32)] * 3
            else:
                found = [state[t, 8 * g : 8 * g + 8, :] for g in range(3)]
            found = gather_tile(
                lambda k, g: table[k, 8 * g : 8 * g + 8, :],
                slot_ref[pl.ds(t, 1), :] - base * LANES,
                8,
                found,
            )
            for g in range(3):
                state[t, 8 * g : 8 * g + 8, :] = found[g]
            return 0

        lax.fori_loop(0, TILES, fetch, 0, unroll=4)

    def row(ref, i):
        return jnp.broadcast_to(ref[i : i + 1, :], (SPECIES, LANES))

    for substep in range(SUB):
        value = jnp.zeros((SPECIES, LANES), jnp.float32)
        for i in range(STEPS):
            value = row(decay_ref, i) * value + row(scale_ref, i) * state[i]
            state[i] = value
        ends = jnp.where(chunk == 0, value + span_all * entry, value)
        for bit in range(6):
            behind = pltpu.roll(ends, 1 << bit, 1)
            ends = jnp.where(chunk >= (1 << bit), ends + levels[bit] * behind, ends)
        before = jnp.where(chunk == 0, entry, pltpu.roll(ends, 1, 1))
        for i in range(STEPS):
            state[i] = state[i] + row(span_ref, i) * before

    def react(j, _):
        base = jnp.concatenate([state[j * 4 + q] for q in range(4)], 1)
        gap = jnp.zeros((8, 4 * LANES), jnp.float32)
        iterate = base
        for _step in range(NEWTON):
            active = jnp.concatenate([jnp.tanh(iterate), gap], 0)
            top = active.astype(jnp.bfloat16)
            rest = (active - top.astype(jnp.float32)).astype(jnp.bfloat16)
            stack = jnp.concatenate([top, rest, top, jnp.zeros_like(top)], 0)
            iterate = base - jnp.dot(inter, stack, preferred_element_type=jnp.float32)
        for q in range(4):
            weight = jnp.broadcast_to(weight_ref[pl.ds(j * 4 + q, 1), :], (8, LANES))
            result = iterate[:, q * LANES : (q + 1) * LANES]
            groups = to_groups(*[result[8 * g : 8 * g + 8] * weight for g in range(3)])
            groups = (jnp.where(row_ids() == 6, weight, groups[0]),) + groups[1:]
            for g in range(4):
                rows[j * 4 + q, 8 * g : 8 * g + 8, :] = groups[g]
        return 0

    lax.fori_loop(0, TILES // 4, react, 0, unroll=2)

    sent(send1, send1_sem)
    for half in range(2):
        ys = [lax.rem(my_y + r, 4) for r in ORDER[2 * half : 2 * half + 2]]
        highs = [y * 4 + sub for y in ys for sub in range(4)]
        total = None
        for j in range(TILES // 4):
            span = range(4 * j, 4 * j + 4)
            left = expand([rows[t] for t in span], [slot_ref[t : t + 1, :] for t in span], highs)
            more = contract(left, [hot_slot[t] for t in span])
            if j == 0:
                acc[0:LOW, :] = more
            else:
                acc[0:LOW, :] += more
        for k in range(8):
            for side in range(2):
                lanes = slice(side * LANES, (side + 1) * LANES)
                blocks = swap_blocks(
                    [acc[k * 32 + 8 * g : k * 32 + 8 * g + 8, lanes] for g in range(4)]
                )
                for d in range(4):
                    send2[highs[k] * 8 + side * 4 + d] = blocks[d][:7]
        for r in ORDER[2 * half : 2 * half + 2]:
            post(send2, recv2, send2_sem, recv2_sem, r)

    for step, r in enumerate(ORDER):
        base = arrived(recv2, recv2_sem, r) * 8
        pad = jnp.zeros((1, LANES), jnp.float32)
        indices = request_ref[pl.ds(pl.multiple_of(base, 8), 8), :]
        for j in range(2):
            tiles = []
            for u in range(4 * j, 4 * j + 4):
                parts = [
                    jnp.concatenate([recv2[base * 4 + u * 4 + d], pad], 0) for d in range(4)
                ]
                tiles.append(jnp.concatenate(swap_blocks(parts), 0))
            span = range(4 * j, 4 * j + 4)
            left = expand(tiles, [indices[u : u + 1] for u in span], range(HIGH))
            more = contract(left, [hot_request[base + u] for u in span])
            if step == 0 and j == 0:
                acc[...] = more
            else:
                acc[...] += more

    for h in range(HIGH):
        for half in range(2):
            lanes = slice(half * LANES, (half + 1) * LANES)
            groups = [acc[h * 32 + 8 * g : h * 32 + 8 * g + 8, lanes] for g in range(4)]
            cells = slice((h * 2 + half) * LANES, (h * 2 + half + 1) * LANES)
            for g, value in enumerate(from_groups(*groups)):
                part[8 * g : 8 * g + 8, cells] = value
            part_flux[:, cells] = groups[0][6:7]

    posts = []
    for k in (2, 1, 3):
        peer = lax.rem(mine + k, BUNDLES)
        cells = pl.ds(pl.multiple_of(peer * QUARTER, QUARTER), QUARTER)
        for source, target, sends, recvs in (
            (part, got, send3_sem, recv3_sem),
            (part_flux, got_flux, send4_sem, recv4_sem),
        ):
            copy = pltpu.make_async_remote_copy(
                src_ref=source.at[:, cells],
                dst_ref=target.at[k - 1],
                send_sem=sends.at[k - 1],
                recv_sem=recvs.at[k - 1],
                device_id=(me, peer),
                device_id_type=MESH,
            )
            copy.start()
            posts.append(copy)
    sent(send2, send2_sem)
    for copy in posts:
        copy.wait()
    ours = pl.ds(pl.multiple_of(mine * QUARTER, QUARTER), QUARTER)
    total = part[:, ours] + got[0] + got[1] + got[2]
    flux = part_flux[:, ours] + got_flux[0] + got_flux[1] + got_flux[2]
    pore = pore_ref[:, ours]
    out_ref[:, ours] = (pore * cell_ref[:, ours] + total) / (pore + flux)
    posts = []
    for k in (2, 1, 3):
        copy = pltpu.make_async_remote_copy(
            src_ref=out_ref.at[:, ours],
            dst_ref=out_ref.at[:, ours],
            send_sem=send5_sem.at[k - 1],
            recv_sem=recv5_sem.at[k - 1],
            device_id=(me, lax.rem(mine + k, BUNDLES)),
            device_id_type=MESH,
        )
        copy.start()
        posts.append(copy)
    for copy in posts:
        copy.wait()


def shards(
    cell_state,
    pore_volume,
    request_cell,
    node_slot,
    line_length,
    courant,
    flux_weight,
    inflow,
    interaction,
):
    f32 = jnp.float32
    i32 = jnp.int32
    vmem = pltpu.VMEM
    dma = pltpu.SemaphoreType.DMA
    return pl.pallas_call(
        kernel,
        out_shape=jax.ShapeDtypeStruct((SPECIES, CELLS), f32),
        in_specs=[pl.BlockSpec(memory_space=pl.ANY)] * 9,
        out_specs=pl.BlockSpec(memory_space=pltpu.VMEM),
        scratch_shapes=[
            vmem((SPECIES, CELLS), f32),
            vmem((1, CELLS), f32),
            vmem((CAP, GRID), i32),
            vmem((LINES, NODES), i32),
            vmem((1, LINES), i32),
            vmem((LINES, NODES), f32),
            vmem((LINES, NODES), f32),
            vmem((1, SPECIES), f32),
            vmem((SPECIES, SPECIES), f32),
            vmem((LANES, LANES), i32),
            vmem((LANES, LANES), f32),
            vmem((32, LANES), i32),
            vmem((32, LANES), f32),
            vmem((32, LANES), i32),
            vmem((32, LANES), i32),
            vmem((32, LANES), f32),
            vmem((32, LANES), f32),
            vmem((32, LANES), f32),
            vmem((32, LANES), f32),
            vmem((TILES, LOW, LANES), jnp.bfloat16),
            vmem((TILES, LOW, LANES), jnp.bfloat16),
            vmem((GRID, 6, LANES), f32),
            vmem((GRID, 6, LANES), f32),
            vmem((GRID, 7, LANES), f32),
            vmem((GRID, 7, LANES), f32),
            vmem((8, SPECIES, LANES), f32),
            vmem((TILES, SPECIES, LANES), f32),
            vmem((TILES, 32, LANES), f32),
            vmem((HIGH * 32, LOW), f32),
            vmem((SPECIES, CELLS), f32),
            vmem((1, CELLS), f32),
            vmem((BUNDLES - 1, SPECIES, QUARTER), f32),
            vmem((BUNDLES - 1, 1, QUARTER), f32),
            dma((9,)),
            dma,
            dma,
            dma((4,)),
            dma,
            dma((4,)),
            dma((3,)),
            dma((3,)),
            dma((3,)),
            dma((3,)),
            dma((3,)),
            dma((3,)),
        ],
        compiler_params=pltpu.CompilerParams(collective_id=0, has_side_effects=True),
        name="streamlines",
    )(
        cell_state,
        pore_volume.reshape(1, CELLS),
        jnp.transpose(request_cell[:, 0], (0, 2, 1)),
        node_slot[0],
        line_length,
        courant[0],
        flux_weight[0],
        inflow,
        interaction,
    )


def solution(mesh):
    placed = (
        P(None, "grid"),
        P("grid"),
        P(None, "grid", None, None),
        P("bundle", "grid", None),
        P("bundle", "grid"),
        P("bundle", "grid", None),
        P("bundle", "grid", None),
        P("bundle", None),
        P(),
    )
    return jax.shard_map(
        shards, mesh=mesh, in_specs=placed, out_specs=P(None, "grid"), check_vma=False
    )
```

time: 119 us -> 89.2 us (0.75)
  Pallas kernels: 111 us -> 87.2 us
  local copies, waits for them, and re-layouts: 7.14 us -> 1.77 us
    pallas_call x1, Pallas kernels: 111 us -> 87.2 us  [shards(): pl.pallas_call(kernel, out_shape=jax.ShapeDtypeStruct((SPECIES, CELLS), f...]
    reshape x6 -> x0, local copies, waits for them, and re-layouts: 2.97 us -> none  [the longest x5 2.27 us: by_step(): values.reshape(LINES, CHUNKS, STEPS).transpose(2, 0, 1)]
    unnamed x13 -> x1, local copies, waits for them, and re-layouts: 3.07 us -> 1.77 us
where the time goes in v1:
time: 89.2 us; the launch traced here: 89 us
  Pallas kernels  87.2 us (98%)
  local copies, waits for them, and re-layouts  1.77 us (2%)
    pallas_call x1, Pallas kernels, shards(): pl.pallas_call(kernel, out_shape=jax.ShapeDtypeStruct((SPECIES, CELLS), f...  87.2 us

profile of v1, /device:TPU:1, one launch (start us, length us, event | category | flops | bytes accessed | tf_op | source)
XLA Modules:
  0.0 89.0 jit_solution(13027000226497635766)
XLA Ops:
  0.0 87.2 %streamlines.1 = f32[24,4096]{1,0:T(8,128)} custom-call(f32[24,4096]{1,0:T(8,128)} %cell_hbm.1, f32[1,4096]{1,0:T(1,128)} %bitcast.8, s32[4,32,128]{2,1,0:T(8,128)} %bitcast.7, s32[2,2048]{1,0:T(2,128)} %bitcast.9, s32[1,2]{1,0:T(1,128)} %length_hbm.1, f32[2,2048]{1,0:T(2,128)} %bitcast.10, f32[2,2048]{1,0:T(2,128)} %bitcast.11, f32[1,24]{1,0:T(1,128)} %inflow_hbm.1, ...), custom_call_target="tpu_custom_call" | custom-call | tf_op jit(solution)/shard_map/streamlines/pallas_call | solution.py:509
  87.2 1.8 %copy.11 = f32[24,4096]{1,0:T(8,128)} copy(f32[24,4096]{1,0:T(8,128)} %streamlines.1) | data formatting | bytes 786432

commit v2 on v1

--- a/solution.py
+++ b/solution.py
@@ -65,6 +65,44 @@
     )
 
 
+def to_blocks(v0, v1, v2, flux):
+    row = row_ids()
+    head = row < 5
+    return (
+        jnp.where(head, v0, pltpu.roll(v2, 5, 0)),
+        jnp.where(head, v1, pltpu.roll(v2, 3, 0)),
+        jnp.where(
+            row < 3,
+            pltpu.roll(v0, 3, 0),
+            jnp.where(head, pltpu.roll(v1, 6, 0), pltpu.roll(v2, 1, 0)),
+        ),
+        jnp.where(
+            row < 1,
+            pltpu.roll(v1, 1, 0),
+            jnp.where(head, pltpu.roll(flux, 1, 0), pltpu.roll(v2, 7, 0)),
+        ),
+    )
+
+
+def from_first(g0, g1, g2, g3):
+    row = row_ids()
+    head = row < 5
+    return (
+        jnp.where(head, g0, pltpu.roll(g2, 5, 0)),
+        jnp.where(head, g1, jnp.where(row < 7, pltpu.roll(g2, 2, 0), pltpu.roll(g3, 7, 0))),
+        jnp.where(row < 1, pltpu.roll(g3, 7, 0), 0.0),
+    )
+
+
+def from_second(g0, g1, g2, g3):
+    row = row_ids()
+    return jnp.where(
+        row < 4,
+        jnp.where(row < 2, g0, pltpu.roll(g1, 2, 0)),
+        jnp.where(row < 6, pltpu.roll(g2, 4, 0), pltpu.roll(g3, 6, 0)),
+    )
+
+
 def gather_tile(load, index, count, found):
     lane = jnp.broadcast_to(index & 127, (8, LANES))
     tile = jnp.broadcast_to(index >> 7, (8, LANES))
@@ -81,14 +119,14 @@
     for tile, index in zip(tiles, indices):
         top = tile.astype(jnp.bfloat16).astype(jnp.float32)
         rest = tile - top
-        high = jnp.broadcast_to(index >> 8, (32, LANES))
+        high = jnp.broadcast_to(index >> 8, tile.shape)
         column = [[], []]
         for k in highs:
             here = high == k
-            column[0].append(jnp.where(here, top, 0.0).astype(jnp.bfloat16))
-            column[1].append(jnp.where(here, rest, 0.0).astype(jnp.bfloat16))
-        tops.append(jnp.concatenate(column[0], 0))
-        rests.append(jnp.concatenate(column[1], 0))
+            column[0].append(jnp.where(here, top, 0.0))
+            column[1].append(jnp.where(here, rest, 0.0))
+        tops.append(jnp.concatenate(column[0], 0).astype(jnp.bfloat16))
+        rests.append(jnp.concatenate(column[1], 0).astype(jnp.bfloat16))
     return jnp.concatenate(tops + rests, 1)
 
 
@@ -162,12 +200,16 @@
     hot_request,
     send1,
     recv1,
-    send2,
-    recv2,
+    send_a,
+    recv_a,
+    send_b,
+    recv_b,
     table,
     state,
     rows,
     acc,
+    acc_a,
+    acc_b,
     part,
     part_flux,
     got,
@@ -176,14 +218,20 @@
     own_sem,
     send1_sem,
     recv1_sem,
-    send2_sem,
-    recv2_sem,
+    send_a_sem,
+    recv_a_sem,
+    send_b_sem,
+    recv_b_sem,
     send3_sem,
     recv3_sem,
     send4_sem,
     recv4_sem,
     send5_sem,
     recv5_sem,
+    send6_sem,
+    recv6_sem,
+    send7_sem,
+    recv7_sem,
 ):
     me = lax.axis_index("grid")
     mine = lax.axis_index("bundle")
@@ -241,9 +289,6 @@
             send1[t * 4 + d] = blocks[d][:6]
         return 0
 
-    lax.fori_loop(0, TILES, pick, 0, unroll=2)
-    pl.semaphore_wait(barrier, GRID - 1 + BUNDLES - 1)
-
     def post_one(source, target, send_sem, recv_sem, peer):
         pltpu.make_async_remote_copy(
             src_ref=source.at[peer],
@@ -282,7 +327,11 @@
         blocks = pl.ds(0, GRID - 1)
         pltpu.make_async_copy(source.at[blocks], source.at[blocks], send_sem).wait()
 
-    for r in ORDER:
+    for step, r in enumerate(ORDER):
+        first = lax.rem(my_y + r, 4) * 8
+        lax.fori_loop(0, 8, lambda t, c, first=first: pick(first + t, c), 0, unroll=2)
+        if step == 0:
+            pl.semaphore_wait(barrier, GRID - 1 + BUNDLES - 1)
         post(send1, recv1, send1_sem, recv1_sem, r)
 
     for load in loads[2:]:
@@ -389,13 +438,12 @@
         for q in range(4):
             weight = jnp.broadcast_to(weight_ref[pl.ds(j * 4 + q, 1), :], (8, LANES))
             result = iterate[:, q * LANES : (q + 1) * LANES]
-            groups = to_groups(*[result[8 * g : 8 * g + 8] * weight for g in range(3)])
-            groups = (jnp.where(row_ids() == 6, weight, groups[0]),) + groups[1:]
-            for g in range(4):
-                rows[j * 4 + q, 8 * g : 8 * g + 8, :] = groups[g]
+            for g in range(3):
+                rows[j * 4 + q, 8 * g : 8 * g + 8, :] = result[8 * g : 8 * g + 8] * weight
+            rows[j * 4 + q, 24:32, :] = jnp.where(row_ids() == 0, weight, 0.0)
         return 0
 
-    lax.fori_loop(0, TILES // 4, react, 0, unroll=2)
+    lax.fori_loop(0, TILES // 4, react, 0, unroll=4)
 
     sent(send1, send1_sem)
     for half in range(2):
@@ -414,80 +462,109 @@
             for side in range(2):
                 lanes = slice(side * LANES, (side + 1) * LANES)
                 blocks = swap_blocks(
-                    [acc[k * 32 + 8 * g : k * 32 + 8 * g + 8, lanes] for g in range(4)]
+                    to_blocks(*[acc[k * 32 + 8 * g : k * 32 + 8 * g + 8, lanes] for g in range(4)])
                 )
                 for d in range(4):
-                    send2[highs[k] * 8 + side * 4 + d] = blocks[d][:7]
+                    send_a[highs[k] * 8 + side * 4 + d] = blocks[d][:5]
+                    send_b[highs[k] * 8 + side * 4 + d] = blocks[d][5:7]
         for r in ORDER[2 * half : 2 * half + 2]:
-            post(send2, recv2, send2_sem, recv2_sem, r)
-
-    for step, r in enumerate(ORDER):
-        base = arrived(recv2, recv2_sem, r) * 8
-        pad = jnp.zeros((1, LANES), jnp.float32)
+            post(send_a, recv_a, send_a_sem, recv_a_sem, r)
+    for r in ORDER:
+        post(send_b, recv_b, send_b_sem, recv_b_sem, r)
+
+    def collect(target, recv_sems, step, pad_rows, combine, total):
+        base = arrived(target, recv_sems, ORDER[step]) * 8
+        pad = jnp.zeros((pad_rows, LANES), jnp.float32)
         indices = request_ref[pl.ds(pl.multiple_of(base, 8), 8), :]
         for j in range(2):
+            span = range(4 * j, 4 * j + 4)
             tiles = []
-            for u in range(4 * j, 4 * j + 4):
+            for u in span:
                 parts = [
-                    jnp.concatenate([recv2[base * 4 + u * 4 + d], pad], 0) for d in range(4)
+                    jnp.concatenate([target[base * 4 + u * 4 + d], pad], 0) for d in range(4)
                 ]
-                tiles.append(jnp.concatenate(swap_blocks(parts), 0))
-            span = range(4 * j, 4 * j + 4)
+                tiles.append(combine(*swap_blocks(parts)))
             left = expand(tiles, [indices[u : u + 1] for u in span], range(HIGH))
             more = contract(left, [hot_request[base + u] for u in span])
             if step == 0 and j == 0:
-                acc[...] = more
+                total[...] = more
             else:
-                acc[...] += more
-
+                total[...] += more
+
+    def over_bundles(pairs):
+        copies = []
+        for k in (2, 1, 3):
+            peer = lax.rem(mine + k, BUNDLES)
+            cells = pl.ds(pl.multiple_of(peer * QUARTER, QUARTER), QUARTER)
+            for source, target, sends, recvs in pairs:
+                copy = pltpu.make_async_remote_copy(
+                    src_ref=source(cells),
+                    dst_ref=target(k - 1),
+                    send_sem=sends.at[k - 1],
+                    recv_sem=recvs.at[k - 1],
+                    device_id=(me, peer),
+                    device_id_type=MESH,
+                )
+                copy.start()
+                copies.append(copy)
+        return copies
+
+    ours = pl.ds(pl.multiple_of(mine * QUARTER, QUARTER), QUARTER)
+
+    def finish(species, sends, recvs):
+        total = part[species, ours] + got[0, species] + got[1, species] + got[2, species]
+        flux = part_flux[:, ours] + got_flux[0] + got_flux[1] + got_flux[2]
+        pore = pore_ref[:, ours]
+        out_ref[species, ours] = (pore * cell_ref[species, ours] + total) / (pore + flux)
+        return over_bundles(
+            [
+                (
+                    lambda cells: out_ref.at[species, ours],
+                    lambda k: out_ref.at[species, ours],
+                    sends,
+                    recvs,
+                )
+            ]
+        )
+
+    first = slice(0, 16)
+    second = slice(16, 24)
+    for step in range(4):
+        collect(
+            recv_a, recv_a_sem, step, 3, lambda *g: jnp.concatenate(from_first(*g), 0), acc_a
+        )
     for h in range(HIGH):
-        for half in range(2):
-            lanes = slice(half * LANES, (half + 1) * LANES)
-            groups = [acc[h * 32 + 8 * g : h * 32 + 8 * g + 8, lanes] for g in range(4)]
-            cells = slice((h * 2 + half) * LANES, (h * 2 + half + 1) * LANES)
-            for g, value in enumerate(from_groups(*groups)):
-                part[8 * g : 8 * g + 8, cells] = value
-            part_flux[:, cells] = groups[0][6:7]
-
-    posts = []
-    for k in (2, 1, 3):
-        peer = lax.rem(mine + k, BUNDLES)
-        cells = pl.ds(pl.multiple_of(peer * QUARTER, QUARTER), QUARTER)
-        for source, target, sends, recvs in (
-            (part, got, send3_sem, recv3_sem),
-            (part_flux, got_flux, send4_sem, recv4_sem),
-        ):
-            copy = pltpu.make_async_remote_copy(
-                src_ref=source.at[:, cells],
-                dst_ref=target.at[k - 1],
-                send_sem=sends.at[k - 1],
-                recv_sem=recvs.at[k - 1],
-                device_id=(me, peer),
-                device_id_type=MESH,
-            )
-            copy.start()
-            posts.append(copy)
-    sent(send2, send2_sem)
-    for copy in posts:
+        for side in range(2):
+            lanes = slice(side * LANES, (side + 1) * LANES)
+            cells = slice((h * 2 + side) * LANES, (h * 2 + side + 1) * LANES)
+            part[0:16, cells] = acc_a[h * 24 : h * 24 + 16, lanes]
+            part_flux[:, cells] = acc_a[h * 24 + 16 : h * 24 + 17, lanes]
+    sums_first = over_bundles(
+        [
+            (lambda cells: part.at[first, cells], lambda k: got.at[k, first], send3_sem, recv3_sem),
+            (lambda cells: part_flux.at[:, cells], lambda k: got_flux.at[k], send4_sem, recv4_sem),
+        ]
+    )
+
+    for step in range(4):
+        collect(recv_b, recv_b_sem, step, 6, from_second, acc_b)
+    for h in range(HIGH):
+        for side in range(2):
+            cells = slice((h * 2 + side) * LANES, (h * 2 + side + 1) * LANES)
+            part[second, cells] = acc_b[h * 8 : h * 8 + 8, side * LANES : (side + 1) * LANES]
+    sums_second = over_bundles(
+        [(lambda cells: part.at[second, cells], lambda k: got.at[k, second], send6_sem, recv6_sem)]
+    )
+
+    for copy in sums_first:
         copy.wait()
-    ours = pl.ds(pl.multiple_of(mine * QUARTER, QUARTER), QUARTER)
-    total = part[:, ours] + got[0] + got[1] + got[2]
-    flux = part_flux[:, ours] + got_flux[0] + got_flux[1] + got_flux[2]
-    pore = pore_ref[:, ours]
-    out_ref[:, ours] = (pore * cell_ref[:, ours] + total) / (pore + flux)
-    posts = []
-    for k in (2, 1, 3):
-        copy = pltpu.make_async_remote_copy(
-            src_ref=out_ref.at[:, ours],
-            dst_ref=out_ref.at[:, ours],
-            send_sem=send5_sem.at[k - 1],
-            recv_sem=recv5_sem.at[k - 1],
-            device_id=(me, lax.rem(mine + k, BUNDLES)),
-            device_id_type=MESH,
-        )
-        copy.start()
-        posts.append(copy)
-    for copy in posts:
+    done = finish(first, send5_sem, recv5_sem)
+    for copy in sums_second:
+        copy.wait()
+    done = done + finish(second, send7_sem, recv7_sem)
+    sent(send_a, send_a_sem)
+    sent(send_b, send_b_sem)
+    for copy in done:
         copy.wait()
 
 
@@ -535,12 +612,16 @@
             vmem((TILES, LOW, LANES), jnp.bfloat16),
             vmem((GRID, 6, LANES), f32),
             vmem((GRID, 6, LANES), f32),
-            vmem((GRID, 7, LANES), f32),
-            vmem((GRID, 7, LANES), f32),
+            vmem((GRID, 5, LANES), f32),
+            vmem((GRID, 5, LANES), f32),
+            vmem((GRID, 2, LANES), f32),
+            vmem((GRID, 2, LANES), f32),
             vmem((8, SPECIES, LANES), f32),
             vmem((TILES, SPECIES, LANES), f32),
             vmem((TILES, 32, LANES), f32),
-            vmem((HIGH * 32, LOW), f32),
+            vmem((LOW, LOW), f32),
+            vmem((HIGH * 24, LOW), f32),
+            vmem((HIGH * 8, LOW), f32),
             vmem((SPECIES, CELLS), f32),
             vmem((1, CELLS), f32),
             vmem((BUNDLES - 1, SPECIES, QUARTER), f32),
@@ -551,6 +632,12 @@
             dma((4,)),
             dma,
             dma((4,)),
+            dma,
+            dma((4,)),
+            dma((3,)),
+            dma((3,)),
+            dma((3,)),
+            dma((3,)),
             dma((3,)),
             dma((3,)),
             dma((3,)),

time: 89.2 us -> 84.9 us (0.952)
  Pallas kernels: 87.2 us -> 83 us
    pallas_call x1, Pallas kernels: 87.2 us -> 83 us  [shards(): pl.pallas_call(kernel, out_shape=jax.ShapeDtypeStruct((SPECIES, CELLS), f...]
where the time goes in v2:
time: 84.9 us; the launch traced here: 84.7 us
  Pallas kernels  83 us (98%)
  local copies, waits for them, and re-layouts  1.77 us (2%)
    pallas_call x1, Pallas kernels, shards(): pl.pallas_call(kernel, out_shape=jax.ShapeDtypeStruct((SPECIES, CELLS), f...  83 us
    unnamed x1, local copies, waits for them, and re-layouts  1.77 us

profile of v2, /device:TPU:1, one launch (start us, length us, event | category | flops | bytes accessed | tf_op | source)
XLA Modules:
  0.0 84.7 jit_solution(838456569557328302)
XLA Ops:
  0.0 83.0 %streamlines.1 = f32[24,4096]{1,0:T(8,128)} custom-call(f32[24,4096]{1,0:T(8,128)} %cell_hbm.1, f32[1,4096]{1,0:T(1,128)} %bitcast.8, s32[4,32,128]{2,1,0:T(8,128)} %bitcast.7, s32[2,2048]{1,0:T(2,128)} %bitcast.9, s32[1,2]{1,0:T(1,128)} %length_hbm.1, f32[2,2048]{1,0:T(2,128)} %bitcast.10, f32[2,2048]{1,0:T(2,128)} %bitcast.11, f32[1,24]{1,0:T(1,128)} %inflow_hbm.1, ...), custom_call_target="tpu_custom_call" | custom-call | tf_op jit(solution)/shard_map/streamlines/pallas_call | solution.py:586
  83.0 1.8 %copy.11 = f32[24,4096]{1,0:T(8,128)} copy(f32[24,4096]{1,0:T(8,128)} %streamlines.1) | data formatting | bytes 786432

commit v3 on v2

--- a/solution.py
+++ b/solution.py
@@ -103,11 +103,11 @@
     )
 
 
-def gather_tile(load, index, count, found):
+def gather_tile(load, index, tiles, found):
     lane = jnp.broadcast_to(index & 127, (8, LANES))
     tile = jnp.broadcast_to(index >> 7, (8, LANES))
-    for k in range(count):
-        here = tile == k
+    for k, name in enumerate(tiles):
+        here = tile == name
         for g in range(3):
             found[g] = jnp.where(here, jnp.take_along_axis(load(k, g), lane, axis=1), found[g])
     return found
@@ -163,7 +163,8 @@
     )
 
 
-ORDER = (2, 1, 3, 0)
+GROUPS = ((2, 0, 4), (2, 4, 8), (1, 0, 8), (3, 0, 8), (0, 0, 4), (0, 4, 8))
+SPLITS = ((2,), (1,), (3, 0))
 
 
 def kernel(
@@ -236,8 +237,8 @@
     me = lax.axis_index("grid")
     mine = lax.axis_index("bundle")
     my_y = lax.div(me, 32)
-    my_z = lax.rem(lax.div(me, 2), 16)
-    my_core = lax.rem(me, 2)
+    my_pair = lax.rem(lax.div(me, 4), 8)
+    my_seat = lax.rem(me, 4)
 
     loads = [
         pltpu.make_async_copy(source, target, in_sem.at[j])
@@ -281,7 +282,7 @@
         found = gather_tile(
             lambda k, g: cell_ref[8 * g : 8 * g + 8, k * LANES : (k + 1) * LANES],
             request_ref[pl.ds(t, 1), :],
-            TILES,
+            range(TILES),
             [jnp.zeros((8, LANES), jnp.float32)] * 3,
         )
         blocks = swap_blocks(to_groups(*found))
@@ -299,40 +300,49 @@
             device_id_type=MESH,
         ).start()
 
-    def post(source, target, send_sem, recv_sems, r):
-        first = lax.rem(my_y + r, 4) * 32
+    def hop(j):
+        return 4 + lax.div(j + 1, 2) * (1 - 2 * lax.rem(j, 2))
+
+    def tile_to(r, j):
+        return lax.rem(my_y + r, 4) * 8 + lax.rem(my_pair + hop(j), 8)
+
+    def tile_from(r, j):
+        return lax.rem(my_y + 4 - r, 4) * 8 + lax.rem(my_pair + 8 - hop(j), 8)
+
+    def post(source, target, send_sem, recv_sems, group):
+        r, low, high = GROUPS[group]
+        here = r == 0 and high == 8
 
         def ring(j, _):
-            hop = 8 + lax.div(j + 1, 2) * (1 - 2 * lax.rem(j, 2))
-            spot = first + lax.rem(my_z + hop, 16) * 2
-            for core in range(2):
-                post_one(source, target, send_sem, recv_sems.at[r], spot + core)
+            for seat in range(4):
+                post_one(source, target, send_sem, recv_sems.at[group], tile_to(r, j) * 4 + seat)
             return 0
 
-        lax.fori_loop(0, 16 if r else 15, ring, 0)
-        if r == 0:
-            post_one(
-                source, target, send_sem, recv_sems.at[0], first + my_z * 2 + 1 - my_core
-            )
+        lax.fori_loop(low, high - here, ring, 0)
+        if here:
+            for seat in range(1, 4):
+                peer = tile_to(0, 7) * 4 + lax.rem(my_seat + seat, 4)
+                post_one(source, target, send_sem, recv_sems.at[group], peer)
             own = pltpu.make_async_copy(source.at[me], target.at[me], own_sem)
             own.start()
             own.wait()
 
-    def arrived(target, recv_sems, r):
-        blocks = pl.ds(0, 32 if r else 31)
-        pltpu.make_async_copy(target.at[blocks], target.at[blocks], recv_sems.at[r]).wait()
-        return lax.rem(my_y + 4 - r, 4)
+    def arrived(target, recv_sems, group):
+        r, low, high = GROUPS[group]
+        blocks = pl.ds(0, 4 * (high - low) - (r == 0 and high == 8))
+        pltpu.make_async_copy(target.at[blocks], target.at[blocks], recv_sems.at[group]).wait()
+        return [tile_from(r, j) for j in range(low, high)]
 
     def sent(source, send_sem):
         blocks = pl.ds(0, GRID - 1)
         pltpu.make_async_copy(source.at[blocks], source.at[blocks], send_sem).wait()
 
-    for step, r in enumerate(ORDER):
-        first = lax.rem(my_y + r, 4) * 8
-        lax.fori_loop(0, 8, lambda t, c, first=first: pick(first + t, c), 0, unroll=2)
-        if step == 0:
+    for group in range(len(GROUPS)):
+        r, low, high = GROUPS[group]
+        lax.fori_loop(low, high, lambda j, c, r=r: pick(tile_to(r, j), c), 0, unroll=2)
+        if group == 0:
             pl.semaphore_wait(barrier, GRID - 1 + BUNDLES - 1)
-        post(send1, recv1, send1_sem, recv1_sem, r)
+        post(send1, recv1, send1_sem, recv1_sem, group)
 
     for load in loads[2:]:
         load.wait()
@@ -382,25 +392,23 @@
         behind = pltpu.roll(level, 1 << bit, 1)
         level = jnp.where(chunk >= (1 << bit), level * behind, level)
 
-    for step, r in enumerate(ORDER):
-        base = arrived(recv1, recv1_sem, r) * 8
+    for group in range(len(GROUPS)):
+        names = arrived(recv1, recv1_sem, group)
         pad = jnp.zeros((2, LANES), jnp.float32)
-        for u in range(8):
-            parts = [
-                jnp.concatenate([recv1[base * 4 + u * 4 + d], pad], 0) for d in range(4)
-            ]
+        for u, name in enumerate(names):
+            parts = [jnp.concatenate([recv1[name * 4 + d], pad], 0) for d in range(4)]
             for g, value in enumerate(from_groups(*swap_blocks(parts))):
                 table[u, 8 * g : 8 * g + 8, :] = value
 
-        def fetch(t, _, base=base, step=step):
-            if step == 0:
+        def fetch(t, _, names=names, group=group):
+            if group == 0:
                 found = [jnp.zeros((8, LANES), jnp.float32)] * 3
             else:
                 found = [state[t, 8 * g : 8 * g + 8, :] for g in range(3)]
             found = gather_tile(
                 lambda k, g: table[k, 8 * g : 8 * g + 8, :],
-                slot_ref[pl.ds(t, 1), :] - base * LANES,
-                8,
+                slot_ref[pl.ds(t, 1), :],
+                names,
                 found,
             )
             for g in range(3):
@@ -412,21 +420,30 @@
     def row(ref, i):
         return jnp.broadcast_to(ref[i : i + 1, :], (SPECIES, LANES))
 
+    before = None
     for substep in range(SUB):
         value = jnp.zeros((SPECIES, LANES), jnp.float32)
         for i in range(STEPS):
-            value = row(decay_ref, i) * value + row(scale_ref, i) * state[i]
+            held = state[i]
+            if substep > 0:
+                held = held + row(span_ref, i) * before
+            value = row(decay_ref, i) * value + row(scale_ref, i) * held
             state[i] = value
         ends = jnp.where(chunk == 0, value + span_all * entry, value)
         for bit in range(6):
             behind = pltpu.roll(ends, 1 << bit, 1)
             ends = jnp.where(chunk >= (1 << bit), ends + levels[bit] * behind, ends)
         before = jnp.where(chunk == 0, entry, pltpu.roll(ends, 1, 1))
-        for i in range(STEPS):
-            state[i] = state[i] + row(span_ref, i) * before
 
     def react(j, _):
-        base = jnp.concatenate([state[j * 4 + q] for q in range(4)], 1)
+        base = jnp.concatenate(
+            [
+                state[j * 4 + q]
+                + jnp.broadcast_to(span_ref[pl.ds(j * 4 + q, 1), :], (SPECIES, LANES)) * before
+                for q in range(4)
+            ],
+            1,
+        )
         gap = jnp.zeros((8, 4 * LANES), jnp.float32)
         iterate = base
         for _step in range(NEWTON):
@@ -446,19 +463,19 @@
     lax.fori_loop(0, TILES // 4, react, 0, unroll=4)
 
     sent(send1, send1_sem)
-    for half in range(2):
-        ys = [lax.rem(my_y + r, 4) for r in ORDER[2 * half : 2 * half + 2]]
+    for split in SPLITS:
+        ys = [lax.rem(my_y + r, 4) for r in split]
+        height = 128 * len(split)
         highs = [y * 4 + sub for y in ys for sub in range(4)]
-        total = None
         for j in range(TILES // 4):
             span = range(4 * j, 4 * j + 4)
             left = expand([rows[t] for t in span], [slot_ref[t : t + 1, :] for t in span], highs)
             more = contract(left, [hot_slot[t] for t in span])
             if j == 0:
-                acc[0:LOW, :] = more
+                acc[0:height, :] = more
             else:
-                acc[0:LOW, :] += more
-        for k in range(8):
+                acc[0:height, :] += more
+        for k in range(len(highs)):
             for side in range(2):
                 lanes = slice(side * LANES, (side + 1) * LANES)
                 blocks = swap_blocks(
@@ -467,26 +484,24 @@
                 for d in range(4):
                     send_a[highs[k] * 8 + side * 4 + d] = blocks[d][:5]
                     send_b[highs[k] * 8 + side * 4 + d] = blocks[d][5:7]
-        for r in ORDER[2 * half : 2 * half + 2]:
-            post(send_a, recv_a, send_a_sem, recv_a_sem, r)
-    for r in ORDER:
-        post(send_b, recv_b, send_b_sem, recv_b_sem, r)
-
-    def collect(target, recv_sems, step, pad_rows, combine, total):
-        base = arrived(target, recv_sems, ORDER[step]) * 8
+        for group in range(len(GROUPS)):
+            if GROUPS[group][0] in split:
+                post(send_a, recv_a, send_a_sem, recv_a_sem, group)
+    for group in range(len(GROUPS)):
+        post(send_b, recv_b, send_b_sem, recv_b_sem, group)
+
+    def collect(target, recv_sems, group, pad_rows, combine, total):
+        names = arrived(target, recv_sems, group)
         pad = jnp.zeros((pad_rows, LANES), jnp.float32)
-        indices = request_ref[pl.ds(pl.multiple_of(base, 8), 8), :]
-        for j in range(2):
-            span = range(4 * j, 4 * j + 4)
+        for j in range(0, len(names), 4):
+            span = names[j : j + 4]
             tiles = []
-            for u in span:
-                parts = [
-                    jnp.concatenate([target[base * 4 + u * 4 + d], pad], 0) for d in range(4)
-                ]
+            for name in span:
+                parts = [jnp.concatenate([target[name * 4 + d], pad], 0) for d in range(4)]
                 tiles.append(combine(*swap_blocks(parts)))
-            left = expand(tiles, [indices[u : u + 1] for u in span], range(HIGH))
-            more = contract(left, [hot_request[base + u] for u in span])
-            if step == 0 and j == 0:
+            left = expand(tiles, [request_ref[pl.ds(name, 1), :] for name in span], range(HIGH))
+            more = contract(left, [hot_request[name] for name in span])
+            if group == 0 and j == 0:
                 total[...] = more
             else:
                 total[...] += more
@@ -529,9 +544,9 @@
 
     first = slice(0, 16)
     second = slice(16, 24)
-    for step in range(4):
+    for group in range(len(GROUPS)):
         collect(
-            recv_a, recv_a_sem, step, 3, lambda *g: jnp.concatenate(from_first(*g), 0), acc_a
+            recv_a, recv_a_sem, group, 3, lambda *g: jnp.concatenate(from_first(*g), 0), acc_a
         )
     for h in range(HIGH):
         for side in range(2):
@@ -546,8 +561,8 @@
         ]
     )
 
-    for step in range(4):
-        collect(recv_b, recv_b_sem, step, 6, from_second, acc_b)
+    for group in range(len(GROUPS)):
+        collect(recv_b, recv_b_sem, group, 6, from_second, acc_b)
     for h in range(HIGH):
         for side in range(2):
             cells = slice((h * 2 + side) * LANES, (h * 2 + side + 1) * LANES)
@@ -586,7 +601,7 @@
     return pl.pallas_call(
         kernel,
         out_shape=jax.ShapeDtypeStruct((SPECIES, CELLS), f32),
-        in_specs=[pl.BlockSpec(memory_space=pl.ANY)] * 9,
+        in_specs=[pl.BlockSpec(memory_space=pltpu.HBM)] * 9,
         out_specs=pl.BlockSpec(memory_space=pltpu.VMEM),
         scratch_shapes=[
             vmem((SPECIES, CELLS), f32),
@@ -629,11 +644,11 @@
             dma((9,)),
             dma,
             dma,
-            dma((4,)),
+            dma((len(GROUPS),)),
             dma,
-            dma((4,)),
+            dma((len(GROUPS),)),
             dma,
-            dma((4,)),
+            dma((len(GROUPS),)),
             dma((3,)),
             dma((3,)),
             dma((3,)),
@@ -645,18 +660,25 @@
             dma((3,)),
             dma((3,)),
         ],
-        compiler_params=pltpu.CompilerParams(collective_id=0, has_side_effects=True),
+        compiler_params=pltpu.CompilerParams(
+            collective_id=0, has_side_effects=True, vmem_limit_bytes=20 << 20
+        ),
         name="streamlines",
     )(
-        cell_state,
-        pore_volume.reshape(1, CELLS),
-        jnp.transpose(request_cell[:, 0], (0, 2, 1)),
-        node_slot[0],
-        line_length,
-        courant[0],
-        flux_weight[0],
-        inflow,
-        interaction,
+        *[
+            pltpu.with_memory_space_constraint(x, pltpu.HBM)
+            for x in (
+                cell_state,
+                pore_volume.reshape(1, CELLS),
+                jnp.transpose(request_cell[:, 0], (0, 2, 1)),
+                node_slot[0],
+                line_length,
+                courant[0],
+                flux_weight[0],
+                inflow,
+                interaction,
+            )
+        ]
     )
 
 

time: 84.9 us -> 83.4 us (0.982)
  local copies, waits for them, and re-layouts: 1.77 us -> 0.75 us
    unnamed x1, local copies, waits for them, and re-layouts: 1.77 us -> 0.75 us
where the time goes in v3:
time: 83.4 us; the launch traced here: 83.3 us
  Pallas kernels  82.6 us (99%)
    pallas_call x1, Pallas kernels, shards(): pl.pallas_call(kernel, out_shape=jax.ShapeDtypeStruct((SPECIES, CELLS), f...  82.6 us

profile of v3, /device:TPU:1, one launch (start us, length us, event | category | flops | bytes accessed | tf_op | source)
XLA Modules:
  0.0 83.3 jit_solution(11640202724650986451)
XLA Ops:
  0.0 82.6 %streamlines.1 = f32[24,4096]{1,0:T(8,128)S(1)} custom-call(f32[24,4096]{1,0:T(8,128)} %cell_hbm.1, f32[1,4096]{1,0:T(1,128)} %bitcast.8, s32[4,32,128]{2,1,0:T(8,128)} %bitcast.7, s32[2,2048]{1,0:T(2,128)} %bitcast.9, s32[1,2]{1,0:T(1,128)} %length_hbm.1, f32[2,2048]{1,0:T(2,128)} %bitcast.10, f32[2,2048]{1,0:T(2,128)} %bitcast.11, f32[1,24]{1,0:T(1,128)} %inflow_hbm.1, ...), custom_call_target="tpu_custom_call" | custom-call | tf_op jit(solution)/shard_map/streamlines/pallas_call | solution.py:601
  82.6 0.7 copy.11

commit v4 on v3

--- a/solution.py
+++ b/solution.py
@@ -163,7 +163,8 @@
     )
 
 
-GROUPS = ((2, 0, 4), (2, 4, 8), (1, 0, 8), (3, 0, 8), (0, 0, 4), (0, 4, 8))
+GROUPS = ((2, 0, 4), (2, 4, 8), (1, 0, 8), (3, 0, 8), (0, 0, 8))
+ORDER = (2, 1, 3, 0)
 SPLITS = ((2,), (1,), (3, 0))
 
 
@@ -306,9 +307,6 @@
     def tile_to(r, j):
         return lax.rem(my_y + r, 4) * 8 + lax.rem(my_pair + hop(j), 8)
 
-    def tile_from(r, j):
-        return lax.rem(my_y + 4 - r, 4) * 8 + lax.rem(my_pair + 8 - hop(j), 8)
-
     def post(source, target, send_sem, recv_sems, group):
         r, low, high = GROUPS[group]
         here = r == 0 and high == 8
@@ -327,11 +325,14 @@
             own.start()
             own.wait()
 
-    def arrived(target, recv_sems, group):
-        r, low, high = GROUPS[group]
-        blocks = pl.ds(0, 4 * (high - low) - (r == 0 and high == 8))
-        pltpu.make_async_copy(target.at[blocks], target.at[blocks], recv_sems.at[group]).wait()
-        return [tile_from(r, j) for j in range(low, high)]
+    def arrived(target, recv_sems, r):
+        for group, (offset, low, high) in enumerate(GROUPS):
+            if offset == r:
+                blocks = pl.ds(0, 4 * (high - low) - (r == 0))
+                pltpu.make_async_copy(
+                    target.at[blocks], target.at[blocks], recv_sems.at[group]
+                ).wait()
+        return lax.rem(my_y + 4 - r, 4)
 
     def sent(source, send_sem):
         blocks = pl.ds(0, GRID - 1)
@@ -392,23 +393,25 @@
         behind = pltpu.roll(level, 1 << bit, 1)
         level = jnp.where(chunk >= (1 << bit), level * behind, level)
 
-    for group in range(len(GROUPS)):
-        names = arrived(recv1, recv1_sem, group)
+    for step, r in enumerate(ORDER):
+        base = arrived(recv1, recv1_sem, r) * 8
         pad = jnp.zeros((2, LANES), jnp.float32)
-        for u, name in enumerate(names):
-            parts = [jnp.concatenate([recv1[name * 4 + d], pad], 0) for d in range(4)]
+        for u in range(8):
+            parts = [
+                jnp.concatenate([recv1[base * 4 + u * 4 + d], pad], 0) for d in range(4)
+            ]
             for g, value in enumerate(from_groups(*swap_blocks(parts))):
                 table[u, 8 * g : 8 * g + 8, :] = value
 
-        def fetch(t, _, names=names, group=group):
-            if group == 0:
+        def fetch(t, _, base=base, step=step):
+            if step == 0:
                 found = [jnp.zeros((8, LANES), jnp.float32)] * 3
             else:
                 found = [state[t, 8 * g : 8 * g + 8, :] for g in range(3)]
             found = gather_tile(
                 lambda k, g: table[k, 8 * g : 8 * g + 8, :],
-                slot_ref[pl.ds(t, 1), :],
-                names,
+                slot_ref[pl.ds(t, 1), :] - base * LANES,
+                range(8),
                 found,
             )
             for g in range(3):
@@ -434,16 +437,11 @@
             behind = pltpu.roll(ends, 1 << bit, 1)
             ends = jnp.where(chunk >= (1 << bit), ends + levels[bit] * behind, ends)
         before = jnp.where(chunk == 0, entry, pltpu.roll(ends, 1, 1))
+    for i in range(STEPS):
+        state[i] = state[i] + row(span_ref, i) * before
 
     def react(j, _):
-        base = jnp.concatenate(
-            [
-                state[j * 4 + q]
-                + jnp.broadcast_to(span_ref[pl.ds(j * 4 + q, 1), :], (SPECIES, LANES)) * before
-                for q in range(4)
-            ],
-            1,
-        )
+        base = jnp.concatenate([state[j * 4 + q] for q in range(4)], 1)
         gap = jnp.zeros((8, 4 * LANES), jnp.float32)
         iterate = base
         for _step in range(NEWTON):
@@ -490,18 +488,21 @@
     for group in range(len(GROUPS)):
         post(send_b, recv_b, send_b_sem, recv_b_sem, group)
 
-    def collect(target, recv_sems, group, pad_rows, combine, total):
-        names = arrived(target, recv_sems, group)
+    def collect(target, recv_sems, step, pad_rows, combine, total):
+        base = arrived(target, recv_sems, ORDER[step]) * 8
         pad = jnp.zeros((pad_rows, LANES), jnp.float32)
-        for j in range(0, len(names), 4):
-            span = names[j : j + 4]
+        indices = request_ref[pl.ds(pl.multiple_of(base, 8), 8), :]
+        for j in range(2):
+            span = range(4 * j, 4 * j + 4)
             tiles = []
-            for name in span:
-                parts = [jnp.concatenate([target[name * 4 + d], pad], 0) for d in range(4)]
+            for u in span:
+                parts = [
+                    jnp.concatenate([target[base * 4 + u * 4 + d], pad], 0) for d in range(4)
+                ]
                 tiles.append(combine(*swap_blocks(parts)))
-            left = expand(tiles, [request_ref[pl.ds(name, 1), :] for name in span], range(HIGH))
-            more = contract(left, [hot_request[name] for name in span])
-            if group == 0 and j == 0:
+            left = expand(tiles, [indices[u : u + 1] for u in span], range(HIGH))
+            more = contract(left, [hot_request[base + u] for u in span])
+            if step == 0 and j == 0:
                 total[...] = more
             else:
                 total[...] += more
@@ -544,9 +545,9 @@
 
     first = slice(0, 16)
     second = slice(16, 24)
-    for group in range(len(GROUPS)):
+    for step in range(4):
         collect(
-            recv_a, recv_a_sem, group, 3, lambda *g: jnp.concatenate(from_first(*g), 0), acc_a
+            recv_a, recv_a_sem, step, 3, lambda *g: jnp.concatenate(from_first(*g), 0), acc_a
         )
     for h in range(HIGH):
         for side in range(2):
@@ -561,8 +562,8 @@
         ]
     )
 
-    for group in range(len(GROUPS)):
-        collect(recv_b, recv_b_sem, group, 6, from_second, acc_b)
+    for step in range(4):
+        collect(recv_b, recv_b_sem, step, 6, from_second, acc_b)
     for h in range(HIGH):
         for side in range(2):
             cells = slice((h * 2 + side) * LANES, (h * 2 + side + 1) * LANES)

time: 83.4 us -> 82.1 us (0.984)
  Pallas kernels: 82.6 us -> 81.2 us
    pallas_call x1, Pallas kernels: 82.6 us -> 81.2 us  [shards(): pl.pallas_call(kernel, out_shape=jax.ShapeDtypeStruct((SPECIES, CELLS), f...]
where the time goes in v4:
time: 82.1 us; the launch traced here: 82 us
  Pallas kernels  81.2 us (99%)
    pallas_call x1, Pallas kernels, shards(): pl.pallas_call(kernel, out_shape=jax.ShapeDtypeStruct((SPECIES, CELLS), f...  81.2 us

profile of v4, /device:TPU:1, one launch (start us, length us, event | category | flops | bytes accessed | tf_op | source)
XLA Modules:
  0.0 82.0 jit_solution(2738234966033325114)
XLA Ops:
  0.0 81.2 %streamlines.1 = f32[24,4096]{1,0:T(8,128)S(1)} custom-call(f32[24,4096]{1,0:T(8,128)} %cell_hbm.1, f32[1,4096]{1,0:T(1,128)} %bitcast.8, s32[4,32,128]{2,1,0:T(8,128)} %bitcast.7, s32[2,2048]{1,0:T(2,128)} %bitcast.9, s32[1,2]{1,0:T(1,128)} %length_hbm.1, f32[2,2048]{1,0:T(2,128)} %bitcast.10, f32[2,2048]{1,0:T(2,128)} %bitcast.11, f32[1,24]{1,0:T(1,128)} %inflow_hbm.1, ...), custom_call_target="tpu_custom_call" | custom-call | tf_op jit(solution)/shard_map/streamlines/pallas_call | solution.py:602
  81.2 0.7 copy.11

commit v5 on v4

--- a/solution.py
+++ b/solution.py
@@ -257,22 +257,37 @@
             )
         )
     ]
-    for load in loads:
+    for load in loads[:2]:
         load.start()
 
     barrier = pltpu.get_barrier_semaphore()
 
-    def greet(k, _):
-        pl.semaphore_signal(
-            barrier, inc=1, device_id=(lax.rem(me + k, GRID), mine), device_id_type=MESH
-        )
-        return 0
-
-    lax.fori_loop(1, GRID, greet, 0)
+    def hop(j):
+        return 4 + lax.div(j + 1, 2) * (1 - 2 * lax.rem(j, 2))
+
+    def tile_to(r, j):
+        return lax.rem(my_y + r, 4) * 8 + lax.rem(my_pair + hop(j), 8)
+
+    def signal(peer):
+        pl.semaphore_signal(barrier, inc=1, device_id=(peer, mine), device_id_type=MESH)
+
+    for r in ORDER:
+
+        def greet(j, _, r=r):
+            for seat in range(4):
+                signal(tile_to(r, j) * 4 + seat)
+            return 0
+
+        lax.fori_loop(0, 8 if r else 7, greet, 0)
+    for seat in range(1, 4):
+        signal(tile_to(0, 7) * 4 + lax.rem(my_seat + seat, 4))
     for k in range(1, BUNDLES):
         pl.semaphore_signal(
             barrier, inc=1, device_id=(me, lax.rem(mine + k, BUNDLES)), device_id_type=MESH
         )
+
+    for load in loads[2:]:
+        load.start()
 
     loads[0].wait()
     square_i[:, 0:32] = jnp.transpose(request_in[...], (1, 0))
@@ -300,12 +315,6 @@
             device_id=(peer, mine),
             device_id_type=MESH,
         ).start()
-
-    def hop(j):
-        return 4 + lax.div(j + 1, 2) * (1 - 2 * lax.rem(j, 2))
-
-    def tile_to(r, j):
-        return lax.rem(my_y + r, 4) * 8 + lax.rem(my_pair + hop(j), 8)
 
     def post(source, target, send_sem, recv_sems, group):
         r, low, high = GROUPS[group]

time: 82.1 us -> 81.1 us (0.988)
  Pallas kernels: 81.2 us -> 80.2 us
    pallas_call x1, Pallas kernels: 81.2 us -> 80.2 us  [shards(): pl.pallas_call(kernel, out_shape=jax.ShapeDtypeStruct((SPECIES, CELLS), f...]
where the time goes in v5:
time: 81.1 us; the launch traced here: 81 us
  Pallas kernels  80.2 us (99%)
    pallas_call x1, Pallas kernels, shards(): pl.pallas_call(kernel, out_shape=jax.ShapeDtypeStruct((SPECIES, CELLS), f...  80.2 us

profile of v5, /device:TPU:1, one launch (start us, length us, event | category | flops | bytes accessed | tf_op | source)
XLA Modules:
  0.0 81.0 jit_solution(15274946814867271030)
XLA Ops:
  0.0 80.2 %streamlines.1 = f32[24,4096]{1,0:T(8,128)S(1)} custom-call(f32[24,4096]{1,0:T(8,128)} %cell_hbm.1, f32[1,4096]{1,0:T(1,128)} %bitcast.8, s32[4,32,128]{2,1,0:T(8,128)} %bitcast.7, s32[2,2048]{1,0:T(2,128)} %bitcast.9, s32[1,2]{1,0:T(1,128)} %length_hbm.1, f32[2,2048]{1,0:T(2,128)} %bitcast.10, f32[2,2048]{1,0:T(2,128)} %bitcast.11, f32[1,24]{1,0:T(1,128)} %inflow_hbm.1, ...), custom_call_target="tpu_custom_call" | custom-call | tf_op jit(solution)/shard_map/streamlines/pallas_call | solution.py:611
  80.2 0.7 copy.11
